TPU v7x, 32 devices: a whole 2x2x4 slice. The times are simulated.
32 devices in a mesh: expert: 4 (over y, core), dp: 8 (over z, x).
Axes of the slice: x: 2, y: 2, z: 4, core: 2. Of those that a mesh axis runs over, the one named last changes fastest.
Arguments:
- tokens: bfloat16 [32768, 2048], P(('expert', 'dp')), may hold values from -6 to 6
- block_expert: int32 [256, 1], P(('expert', 'dp')), may hold values from 0 to 3; in each aligned block of 8 rows (0 to 7, 8 to 15, ...) at most 4 rows name the same one
- gate_weight: bfloat16 [4, 2048, 768], P('expert', 'dp'), may hold values from -0.125 to 0.125
- up_weight: bfloat16 [4, 2048, 768], P('expert', 'dp'), may hold values from -0.125 to 0.125
- down_weight: bfloat16 [4, 768, 2048], P('expert', None, 'dp'), may hold values from -0.21875 to 0.21875
Outputs:
- r_factor: float32 [4, 768, 768], P('expert', 'dp')
- compressed_down: float32 [4, 768, 2048], P('expert', None, 'dp')
Inputs may be any that keep to these rules, and one draw needn't show every extreme that they name: `block_expert`: among the 8 blocks of one device, at most 4 name the same expert, and in every draw some device has exactly 4 blocks for one expert.
All inputs are finite; a program needn't handle non-finite values.
Results may differ from a plain program's by a relative error of at most 0.0003.
Values may be sent and summed in bfloat16 or wider, within the bound.
No kernel may reach another device: no remote copies, remote signals or barrier semaphores. Data moves between devices by JAX's collectives and lax.ppermute only.
A program may use at most 128 MiB of HBM per device.

v0:
```python
import jax
import jax.numpy as jnp
from jax import lax
from jax.sharding import PartitionSpec as P

BROWS = 128
damping = 0.05


def on_device(tokens, block_expert, gate_weight, up_weight, down_weight):
    n_expert = lax.axis_size("expert")
    n_data = lax.axis_size("dp")
    exp_local = gate_weight.shape[0]
    width = gate_weight.shape[2]
    model = tokens.shape[1]
    experts = exp_local * n_expert
    blk_count = block_expert.shape[0]
    capacity = max(2, 2 * blk_count // experts)
    rows_avg = blk_count * BROWS * n_data * n_expert // experts
    blocks = tokens.reshape(blk_count, BROWS, model)
    ids = block_expert[:, 0]
    positions = jnp.arange(blk_count, dtype=jnp.int32)
    same = ids[:, None] == ids[None, :]
    earlier = positions[None, :] < positions[:, None]
    ranks = jnp.sum((same & earlier).astype(jnp.int32), axis=1)
    slots = jnp.arange(experts * capacity, dtype=jnp.int32)
    match = (ids[None, :] == (slots // capacity)[:, None]) & (
        ranks[None, :] == (slots % capacity)[:, None]
    )
    found = jnp.sum(match.astype(jnp.int32), axis=1)
    source = jnp.sum(match.astype(jnp.int32) * positions[None, :], axis=1) + (1 - found) * blk_count
    padded = jnp.concatenate([blocks, jnp.zeros((1, BROWS, model), jnp.bfloat16)], axis=0)
    outgoing = padded[source].reshape(n_expert, exp_local, capacity, BROWS, model)
    arrived = lax.all_to_all(outgoing, "expert", split_axis=0, concat_axis=0, tiled=True)
    eye = jnp.eye(width, dtype=jnp.float32)
    my_rows = width // n_data
    rows = arrived[:, 0].reshape(-1, model)
    gate = jnp.dot(
        rows,
        lax.all_gather(gate_weight[0], "dp", axis=0, tiled=True),
        preferred_element_type=jnp.float32,
    )
    lifted = jnp.dot(
        rows,
        lax.all_gather(up_weight[0], "dp", axis=0, tiled=True),
        preferred_element_type=jnp.float32,
    )
    hidden = jax.nn.silu(gate) * lifted
    gram = jnp.dot(hidden.T, hidden, precision=lax.Precision.HIGHEST) / float(rows_avg)
    total = lax.psum(gram, "dp") + damping * eye
    upper = jnp.linalg.cholesky(total).T
    factors = [lax.dynamic_slice_in_dim(upper, lax.axis_index("dp") * my_rows, my_rows, 0)]
    products = [jnp.dot(upper, down_weight[0].astype(jnp.float32), precision=lax.Precision.HIGHEST)]
    return (jnp.stack(factors), jnp.stack(products))


def solution(mesh):
    placed = (
        P(("expert", "dp"), None),
        P(("expert", "dp"), None),
        P("expert", "dp", None),
        P("expert", "dp", None),
        P("expert", None, "dp"),
    )
    return jax.shard_map(
        on_device,
        mesh=mesh,
        in_specs=placed,
        out_specs=(P("expert", "dp", None), P("expert", None, "dp")),
        check_vma=False,
    )
```

profile of v0, /device:TPU:0, one launch (start us, length us, event | category | flops | bytes accessed | tf_op | source)
XLA Modules:
  0.0 432.7 jit_solution(1642863032886914557)
XLA Ops:
  7.2 0.0 copy-start
  7.2 0.0 all-gather.7.cloned.1.call-start
  7.2 0.7 all-gather.7.cloned.1.call-update
  7.9 0.0 copy-start.3
  7.9 5.0 %concatenate.3 = bf16[9,128,2048]{2,1,0:T(8,128)(2,1)} pad(bf16[8,128,2048]{2,1,0:T(8,128)(2,1)} %bitcast.59, bf16[]{:T(256)} %constant.236.clone.1), padding=0_1x0_0x0_0 | pad | bytes 8912898 | tf_op jit(solution)/shard_map/concatenate | solution.py:32
  12.9 0.0 copy-done.3
  12.9 0.2 convert_reduce_fusion.1
  13.1 0.1 convert_reduce_fusion
  13.2 7.1 %gather_fusion = bf16[16,128,2048]{2,1,0:T(8,128)(2,1)} fusion(bf16[9,128,2048]{2,1,0:T(8,128)(2,1)} %concatenate.3, s32[1024]{0:T(1024)S(1)} %pad_clamp_fusion), kind=kCustom, calls=%fused_computation | custom fusion | bytes 16777280 | tf_op jit(solution)/shard_map/gather | solution.py:33
  20.3 5.7 %all-to-all-start = ((bf16[4,1,4,128,2048]{4,3,2,1,0:T(8,128)(2,1)}), bf16[4,1,4,128,2048]{4,3,2,1,0:T(8,128)(2,1)}, u32[]{:S(2)}, u32[]{:S(2)}) async-start(bf16[4,1,4,128,2048]{4,3,2,1,0:T(8,128)(2,1)} %bitcast.58), calls=%async_computation | async-start | bytes 16777216 | tf_op jit(solution)/shard_map/all_to_all | solution.py:34
  25.9 0.0 all-gather.5.cloned.1.call-start
  26.0 0.7 all-gather.5.cloned.1.call-update
  26.7 0.0 all-reduce.4.cloned.1.call-start
  26.7 46.2 %all-gather.7.cloned.1.call-done = bf16[1,2048,768]{2,1,0:T(8,128)(2,1)} async-done(((bf16[1,256,768]{2,1,0:T(8,128)(2,1)}), bf16[1,2048,768]{2,1,0:T(8,128)(2,1)}) %all-gather.7.cloned.1.call-update) | async-done | bytes 3145744 | tf_op jit(solution)/shard_map/all_gather | solution.py:45
  72.9 46.9 %all-to-all-done = bf16[4,1,4,128,2048]{4,3,2,1,0:T(8,128)(2,1)} async-done(((bf16[4,1,4,128,2048]{4,3,2,1,0:T(8,128)(2,1)}), bf16[4,1,4,128,2048]{4,3,2,1,0:T(8,128)(2,1)}, u32[]{:S(2)}, u32[]{:S(2)}) %all-to-all-start) | async-done | bytes 8388640 | tf_op jit(solution)/shard_map/all_to_all | solution.py:34
  119.8 11.7 %fusion.7 = f32[2048,768]{1,0:T(8,128)} fusion(bf16[2048,2048]{1,0:T(8,128)(2,1)} %bitcast.5, bf16[1,2048,768]{2,1,0:T(8,128)(2,1)} %all-gather.7.cloned.1.call-done), kind=kOutput, calls=%fused_computation.8 | convolution fusion | flops 6442450944 | bytes 17825792 | tf_op jit(solution)/shard_map/dot_general | solution.py:43
  131.5 2.3 all-gather.5.cloned.1.call-done
  133.8 10.3 %fusion.9 = f32[2048,768]{1,0:T(8,128)S(1)} fusion(bf16[2048,2048]{1,0:T(8,128)(2,1)} %bitcast.5, bf16[1,2048,768]{2,1,0:T(8,128)(2,1)} %all-gather.5.cloned.1.call-done), kind=kOutput, calls=%fused_computation.10 | convolution fusion | flops 6442450944 | bytes 17825792 | tf_op jit(solution)/shard_map/dot_general | solution.py:38
  144.2 0.0 copy-done.4
  144.2 20.1 %fusion.13 = f32[768,768]{0,1:T(8,128)} fusion(f32[2048,768]{1,0:T(8,128)S(1)} %copy-done.4, f32[2048,768]{1,0:T(8,128)S(1)} %fusion.9), kind=kOutput, calls=%fused_computation.19 | convolution fusion | flops 14503968768 | bytes 14942208 | tf_op jit(solution)/shard_map/dot_general | solution.py:49
  164.2 0.0 all-reduce.4.cloned.1.call-update
  164.2 107.7 %all-reduce.4.cloned.1.call-done = f32[768,768]{0,1:T(8,128)} async-done(((f32[768,768]{0,1:T(8,128)}), f32[768,768]{0,1:T(8,128)}) %all-reduce.4.cloned.1.call-update) | async-done | bytes 2359312 | tf_op jit(solution)/shard_map/psum | solution.py:50
  272.0 3.3 select_add_fusion
  275.2 3.2 copy.24
  278.4 0.0 copy-done.1
  278.4 2.0 fusion.12
  280.4 1.4 copy-done.2
  281.8 11.7 %cholesky.164 = f32[128,128]{1,0:T(8,128)S(1)} custom-call(f32[128,128]{1,0:T(8,128)S(1)} %cholesky.421), custom_call_target="Cholesky" | custom-call | tf_op jit(solution)/shard_map/jit(cholesky)/cholesky | solution.py:51
  293.6 0.1 copy.25
  293.7 9.8 %custom-call.43 = f32[1,128,128]{1,2,0:T(8,128)S(1)} custom-call(f32[1,128,128]{2,1,0:T(8,128)S(1)} %get-tuple-element.13), custom_call_target="InvertDiagBlocksLowerTriangular" | custom-call | tf_op jit(solution)/shard_map/jit(cholesky)/cholesky | solution.py:51
  303.5 0.2 cholesky.338
  303.6 1.5 constant_dynamic-update-slice_fusion.4
  305.1 1.7 convolution_subtract_fusion
  306.8 11.7 %cholesky.187 = f32[128,128]{1,0:T(8,128)S(1)} custom-call(f32[128,128]{1,0:T(8,128)S(1)} %cholesky.425), custom_call_target="Cholesky" | custom-call | tf_op jit(solution)/shard_map/jit(cholesky)/cholesky | solution.py:51
  318.5 0.1 copy.26
  318.6 10.0 %custom-call.44 = f32[1,128,128]{1,2,0:T(8,128)S(1)} custom-call(f32[1,128,128]{2,1,0:T(8,128)S(1)} %get-tuple-element.11), custom_call_target="InvertDiagBlocksLowerTriangular" | custom-call | tf_op jit(solution)/shard_map/jit(cholesky)/cholesky | solution.py:51
  328.6 0.4 convolution_dynamic-update-slice_fusion
  329.0 1.9 convolution_subtract_fusion.1
  331.0 11.7 %cholesky.352 = f32[128,128]{1,0:T(8,128)S(1)} custom-call(f32[128,128]{1,0:T(8,128)S(1)} %cholesky.430), custom_call_target="Cholesky" | custom-call | tf_op jit(solution)/shard_map/jit(cholesky)/cholesky | solution.py:51
  342.8 0.1 copy.27
  342.9 9.8 %custom-call.45 = f32[1,128,128]{1,2,0:T(8,128)S(1)} custom-call(f32[1,128,128]{2,1,0:T(8,128)S(1)} %get-tuple-element.9), custom_call_target="InvertDiagBlocksLowerTriangular" | custom-call | tf_op jit(solution)/shard_map/jit(cholesky)/cholesky | solution.py:51
  352.7 0.4 convolution_dynamic-update-slice_fusion.1
  353.1 2.1 convolution_subtract_fusion.2
  355.2 11.9 %cholesky.371 = f32[128,128]{1,0:T(8,128)S(1)} custom-call(f32[128,128]{1,0:T(8,128)S(1)} %cholesky.435), custom_call_target="Cholesky" | custom-call | tf_op jit(solution)/shard_map/jit(cholesky)/cholesky | solution.py:51
  367.1 0.1 copy.28
  367.2 9.8 %custom-call.46 = f32[1,128,128]{1,2,0:T(8,128)S(1)} custom-call(f32[1,128,128]{2,1,0:T(8,128)S(1)} %get-tuple-element.7), custom_call_target="InvertDiagBlocksLowerTriangular" | custom-call | tf_op jit(solution)/shard_map/jit(cholesky)/cholesky | solution.py:51
  377.1 0.3 convolution_dynamic-update-slice_fusion.2
  377.4 1.9 convolution_subtract_fusion.3
  379.3 11.7 %cholesky.390 = f32[128,128]{1,0:T(8,128)S(1)} custom-call(f32[128,128]{1,0:T(8,128)S(1)} %cholesky.440), custom_call_target="Cholesky" | custom-call | tf_op jit(solution)/shard_map/jit(cholesky)/cholesky | solution.py:51
  391.1 0.1 copy.29
  391.2 9.8 %custom-call.47 = f32[1,128,128]{1,2,0:T(8,128)S(1)} custom-call(f32[1,128,128]{2,1,0:T(8,128)S(1)} %get-tuple-element.5), custom_call_target="InvertDiagBlocksLowerTriangular" | custom-call | tf_op jit(solution)/shard_map/jit(cholesky)/cholesky | solution.py:51
  401.0 0.3 convolution_dynamic-update-slice_fusion.3
  401.3 1.8 convolution_subtract_fusion.4
  403.1 11.7 %cholesky.408 = f32[128,128]{1,0:T(8,128)S(1)} custom-call(f32[128,128]{1,0:T(8,128)S(1)} %convolution_subtract_fusion.4), custom_call_target="Cholesky" | custom-call | tf_op jit(solution)/shard_map/jit(cholesky)/cholesky | solution.py:51
  414.8 0.1 copy.30
  414.9 0.6 compare_reduce_fusion.4
  415.6 0.6 compare_reduce_fusion.5
  416.2 0.7 compare_reduce_fusion.3
  416.9 0.6 compare_reduce_fusion.2
  417.5 0.7 compare_reduce_fusion.1
  418.2 0.7 compare_reduce_fusion
  422.7 0.2 select_select_fusion
  422.9 2.1 convolution_bitcast_fusion
  425.0 0.7 dynamic-slice_bitcast_fusion
  (23 shorter events, 0.3 us)
Async XLA Ops:
  7.2 415.7 %copy-start = (bf16[1,768,256]{2,1,0:T(8,128)(2,1)S(1)}, bf16[1,768,256]{2,1,0:T(8,128)(2,1)}, u32[]{:S(2)}) copy-start(bf16[1,768,256]{2,1,0:T(8,128)(2,1)} %param.9) | copy-start | bytes 1179652
  7.2 65.8 %all-gather.7.cloned.1.call-start = ((), (), s32[]{:S(2)}) async-start(), calls=%async_computation.3 | async-start | bytes 3538944 | tf_op jit(solution)/shard_map/all_gather | solution.py:45
  7.9 5.0 %copy-start.3 = (s32[8,1]{0,1:T(1,128)S(1)}, s32[8,1]{0,1:T(1,128)}, u32[]{:S(2)}) copy-start(s32[8,1]{0,1:T(1,128)} %param.6) | copy-start | bytes 100
  20.3 99.5 %all-to-all-start = ((bf16[4,1,4,128,2048]{4,3,2,1,0:T(8,128)(2,1)}), bf16[4,1,4,128,2048]{4,3,2,1,0:T(8,128)(2,1)}, u32[]{:S(2)}, u32[]{:S(2)}) async-start(bf16[4,1,4,128,2048]{4,3,2,1,0:T(8,128)(2,1)} %bitcast.58), calls=%async_computation | async-start | bytes 16777216 | tf_op jit(solution)/shard_map/all_to_all | solution.py:34
  25.9 107.9 %all-gather.5.cloned.1.call-start = ((), (), s32[]{:S(2)}) async-start(), calls=%async_computation.2 | async-start | bytes 3538944 | tf_op jit(solution)/shard_map/all_gather | solution.py:40
  26.7 245.3 %all-reduce.4.cloned.1.call-start = ((), (), s32[]{:S(2)}) async-start(), calls=%async_computation.1 | async-start | bytes 4718592 | tf_op jit(solution)/shard_map/psum | solution.py:50
  133.8 10.3 %copy-start.4 = (f32[2048,768]{1,0:T(8,128)S(1)}, f32[2048,768]{1,0:T(8,128)}, u32[]{:S(2)}) copy-start(f32[2048,768]{1,0:T(8,128)} %fusion.7) | copy-start | bytes 18874372
  275.2 3.2 copy-start.1
  280.4 1.4 copy-start.2
Sparse Core Ops, SparseCore 0:
  10.2 62.7 all-gather.6
  75.1 58.6 all-gather.4
  164.4 107.5 all-reduce.3
where the time goes:
time: 438 us; the launch traced here: 433 us
  waiting for transfers between devices  204 us (47%)
  other arithmetic  130 us (30%)
  matrix products  56.5 us (13%)
  between operations  18.3 us (4%)
  local copies, waits for them, and re-layouts  18.2 us (4%)
  starting transfers between devices  5.77 us (1%)
    another operation x23, other arithmetic, on_device(): upper = jnp.linalg.cholesky(total).T  124 us
    psum x1, waiting for transfers between devices, on_device(): total = lax.psum(gram, 'dp') + damping * eye  108 us
    all_to_all x1, waiting for transfers between devices, on_device(): lax.all_to_all(outgoing, 'expert', split_axis=0, concat_axis=0, tiled=True)  46.9 us
    all_gather x1, waiting for transfers between devices, on_device(): lax.all_gather(up_weight[0], 'dp', axis=0, tiled=True)  46.2 us
    dot_general x1, matrix products, on_device(): jnp.dot(hidden.T, hidden, precision=lax.Precision.HIGHEST) / float(rows_avg)  20.1 us
    another operation x10, matrix products, on_device(): upper = jnp.linalg.cholesky(total).T  12.3 us
    dot_general x1, matrix products, on_device(): jnp.dot(rows, lax.all_gather(up_weight[0], 'dp', axis=0, tiled=True), pre...  11.7 us
    dot_general x1, matrix products, on_device(): jnp.dot(rows, lax.all_gather(gate_weight[0], 'dp', axis=0, tiled=True), p...  10.3 us
  transfers between devices with their start and end apart: 4, of which 4 were waited for; matrix products, arithmetic and copies ran while one was open for 6% of the time, Pallas kernels for 0%

commit v1 on v0

--- a/solution.py
+++ b/solution.py
@@ -5,6 +5,11 @@
 
 BROWS = 128
 damping = 0.05
+
+
+def draft_the_lots_all(piece_in):
+    z_new = jax.lax.all_gather(piece_in, "dp").sum(axis=0)
+    return z_new
 
 
 def on_device(tokens, block_expert, gate_weight, up_weight, down_weight):
@@ -47,7 +52,7 @@
     )
     hidden = jax.nn.silu(gate) * lifted
     gram = jnp.dot(hidden.T, hidden, precision=lax.Precision.HIGHEST) / float(rows_avg)
-    total = lax.psum(gram, "dp") + damping * eye
+    total = draft_the_lots_all(gram) + damping * eye
     upper = jnp.linalg.cholesky(total).T
     factors = [lax.dynamic_slice_in_dim(upper, lax.axis_index("dp") * my_rows, my_rows, 0)]
     products = [jnp.dot(upper, down_weight[0].astype(jnp.float32), precision=lax.Precision.HIGHEST)]

time: 438 us -> 696 us (1.59)
  waiting for transfers between devices: 204 us -> 458 us
    all_gather x0 -> x1, waiting for transfers between devices: none -> 361 us  [draft_the_lots_all(): z_new = jax.lax.all_gather(piece_in, 'dp').sum(axis=0)]
    psum x1 -> x0, waiting for transfers between devices: 108 us -> none  [on_device(): total = lax.psum(gram, 'dp') + damping * eye]
    reduce_sum x0 -> x1, other arithmetic: none -> 7.87 us  [draft_the_lots_all(): z_new = jax.lax.all_gather(piece_in, 'dp').sum(axis=0)]
  transfers between devices with their start and end apart: 4 -> 4, of which waited for: 4 -> 4; matrix products, arithmetic and copies ran while one was open for 6% -> 3% of each run, Pallas kernels for 0% -> 0%
where the time goes in v1:
time: 696 us; the launch traced here: 690 us
  waiting for transfers between devices  458 us (66%)
  other arithmetic  135 us (19%)
  matrix products  54.7 us (8%)
  local copies, waits for them, and re-layouts  18.7 us (3%)
  between operations  18 us (3%)
    all_gather x1, waiting for transfers between devices, draft_the_lots_all(): z_new = jax.lax.all_gather(piece_in, 'dp').sum(axis=0)  361 us
    another operation x23, other arithmetic, on_device(): upper = jnp.linalg.cholesky(total).T  124 us
    all_to_all x1, waiting for transfers between devices, on_device(): lax.all_to_all(outgoing, 'expert', split_axis=0, concat_axis=0, tiled=True)  46.9 us
    all_gather x1, waiting for transfers between devices, on_device(): lax.all_gather(up_weight[0], 'dp', axis=0, tiled=True)  46.2 us
    dot_general x1, matrix products, on_device(): jnp.dot(hidden.T, hidden, precision=lax.Precision.HIGHEST) / float(rows_avg)  19.4 us
  transfers between devices with their start and end apart: 4, of which 4 were waited for; matrix products, arithmetic and copies ran while one was open for 3% of the time, Pallas kernels for 0%

profile of v1, /device:TPU:0, one launch (start us, length us, event | category | flops | bytes accessed | tf_op | source)
XLA Modules:
  0.0 689.9 jit_solution(8153738156929625589)
XLA Ops:
  7.2 0.0 copy-start
  7.2 0.0 all-gather.9.cloned.1.call-start
  7.2 0.7 all-gather.9.cloned.1.call-update
  7.9 0.0 copy-start.2
  7.9 5.0 concatenate.3
  12.9 0.0 copy-done.2
  12.9 0.2 convert_reduce_fusion.1
  13.1 0.1 convert_reduce_fusion
  13.2 7.1 %gather_fusion = bf16[16,128,2048]{2,1,0:T(8,128)(2,1)} fusion(bf16[9,128,2048]{2,1,0:T(8,128)(2,1)} %concatenate.3, s32[1024]{0:T(1024)S(1)} %pad_clamp_fusion), kind=kCustom, calls=%fused_computation | custom fusion | bytes 16777280 | tf_op jit(solution)/shard_map/gather | solution.py:38
  20.3 5.7 all-to-all-start
  25.9 0.0 all-gather.7.cloned.1.call-start
  26.0 0.7 all-gather.7.cloned.1.call-update
  26.7 0.0 all-gather.11.cloned.1.call-start
  26.7 46.2 %all-gather.9.cloned.1.call-done = bf16[1,2048,768]{2,1,0:T(8,128)(2,1)} async-done(((bf16[1,256,768]{2,1,0:T(8,128)(2,1)}), bf16[1,2048,768]{2,1,0:T(8,128)(2,1)}) %all-gather.9.cloned.1.call-update) | async-done | bytes 3145744 | tf_op jit(solution)/shard_map/all_gather | solution.py:50
  72.9 46.9 %all-to-all-done = bf16[4,1,4,128,2048]{4,3,2,1,0:T(8,128)(2,1)} async-done(((bf16[4,1,4,128,2048]{4,3,2,1,0:T(8,128)(2,1)}), bf16[4,1,4,128,2048]{4,3,2,1,0:T(8,128)(2,1)}, u32[]{:S(2)}, u32[]{:S(2)}) %all-to-all-start) | async-done | bytes 8388640 | tf_op jit(solution)/shard_map/all_to_all | solution.py:39
  119.8 11.7 %fusion.7 = f32[2048,768]{1,0:T(8,128)} fusion(bf16[2048,2048]{1,0:T(8,128)(2,1)} %bitcast.5, bf16[1,2048,768]{2,1,0:T(8,128)(2,1)} %all-gather.9.cloned.1.call-done), kind=kOutput, calls=%fused_computation.8 | convolution fusion | flops 6442450944 | bytes 17825792 | tf_op jit(solution)/shard_map/dot_general | solution.py:48
  131.5 2.3 all-gather.7.cloned.1.call-done
  133.8 0.0 copy-start.3
  133.8 10.4 %fusion.9 = f32[2048,768]{1,0:T(8,128)S(1)} fusion(bf16[2048,2048]{1,0:T(8,128)(2,1)} %bitcast.5, bf16[1,2048,768]{2,1,0:T(8,128)(2,1)} %all-gather.7.cloned.1.call-done), kind=kOutput, calls=%fused_computation.10 | convolution fusion | flops 6442450944 | bytes 17825792 | tf_op jit(solution)/shard_map/dot_general | solution.py:43
  144.3 0.0 copy-done.3
  144.3 19.4 %fusion.12 = f32[768,768]{1,0:T(8,128)} fusion(f32[2048,768]{1,0:T(8,128)S(1)} %copy-done.3, f32[2048,768]{1,0:T(8,128)S(1)} %fusion.9), kind=kOutput, calls=%fused_computation.18 | convolution fusion | flops 14503968768 | bytes 14942208 | tf_op jit(solution)/shard_map/dot_general | solution.py:54
  163.7 0.0 all-gather.11.cloned.1.call-update
  163.7 361.5 %all-gather.11.cloned.1.call-done = f32[6144,768]{1,0:T(8,128)} async-done(((f32[768,768]{1,0:T(8,128)}), f32[6144,768]{1,0:T(8,128)}) %all-gather.11.cloned.1.call-update) | async-done | bytes 18874384 | tf_op jit(solution)/shard_map/all_gather | solution.py:11
  525.2 7.9 %reduce_sum.41 = f32[768,768]{1,0:T(8,128)S(1)} reduce(f32[8,768,768]{2,1,0:T(8,128)} %bitcast.56, f32[]{:T(128)} %constant.248.clone.1), dimensions={0}, to_apply=%region_3.4 | reduce | flops 4128768 | bytes 21233668 | tf_op jit(solution)/shard_map/reduce_sum | solution.py:11
  533.1 2.1 copy.21
  535.2 2.0 add_multiply_fusion
  537.2 0.0 copy-start.1
  537.2 1.4 copy-done.1
  538.6 11.7 %cholesky.164 = f32[128,128]{1,0:T(8,128)S(1)} custom-call(f32[128,128]{1,0:T(8,128)S(1)} %cholesky.421), custom_call_target="Cholesky" | custom-call | tf_op jit(solution)/shard_map/jit(cholesky)/cholesky | solution.py:56
  550.4 0.2 cholesky.338
  550.5 9.8 %custom-call.43 = f32[1,128,128]{1,2,0:T(8,128)S(1)} custom-call(f32[1,128,128]{2,1,0:T(8,128)S(1)} %get-tuple-element.25), custom_call_target="InvertDiagBlocksLowerTriangular" | custom-call | tf_op jit(solution)/shard_map/jit(cholesky)/cholesky | solution.py:56
  560.3 1.5 fusion.20
  561.8 0.9 copy.22
  562.7 1.7 convolution_subtract_fusion
  564.4 11.7 %cholesky.187 = f32[128,128]{1,0:T(8,128)S(1)} custom-call(f32[128,128]{1,0:T(8,128)S(1)} %cholesky.425), custom_call_target="Cholesky" | custom-call | tf_op jit(solution)/shard_map/jit(cholesky)/cholesky | solution.py:56
  576.1 1.0 constant_dynamic-update-slice_fusion.4
  577.1 0.6 compare_reduce_fusion.4
  577.8 0.6 compare_reduce_fusion.5
  578.4 10.0 %custom-call.44 = f32[1,128,128]{1,2,0:T(8,128)S(1)} custom-call(f32[1,128,128]{2,1,0:T(8,128)S(1)} %get-tuple-element.22), custom_call_target="InvertDiagBlocksLowerTriangular" | custom-call | tf_op jit(solution)/shard_map/jit(cholesky)/cholesky | solution.py:56
  588.4 0.4 convolution_dynamic-update-slice_fusion
  588.8 1.5 convolution_subtract_fusion.1
  590.3 11.7 %cholesky.352 = f32[128,128]{1,0:T(8,128)S(1)} custom-call(f32[128,128]{1,0:T(8,128)S(1)} %cholesky.430), custom_call_target="Cholesky" | custom-call | tf_op jit(solution)/shard_map/jit(cholesky)/cholesky | solution.py:56
  602.1 0.6 compare_reduce_fusion.3
  602.7 9.8 %custom-call.45 = f32[1,128,128]{1,2,0:T(8,128)S(1)} custom-call(f32[1,128,128]{2,1,0:T(8,128)S(1)} %get-tuple-element.19), custom_call_target="InvertDiagBlocksLowerTriangular" | custom-call | tf_op jit(solution)/shard_map/jit(cholesky)/cholesky | solution.py:56
  612.5 0.3 convolution_dynamic-update-slice_fusion.1
  612.8 1.6 convolution_subtract_fusion.2
  614.4 12.1 %cholesky.371 = f32[128,128]{1,0:T(8,128)S(1)} custom-call(f32[128,128]{1,0:T(8,128)S(1)} %cholesky.435), custom_call_target="Cholesky" | custom-call | tf_op jit(solution)/shard_map/jit(cholesky)/cholesky | solution.py:56
  626.5 0.7 compare_reduce_fusion.2
  627.2 9.8 %custom-call.46 = f32[1,128,128]{1,2,0:T(8,128)S(1)} custom-call(f32[1,128,128]{2,1,0:T(8,128)S(1)} %get-tuple-element.16), custom_call_target="InvertDiagBlocksLowerTriangular" | custom-call | tf_op jit(solution)/shard_map/jit(cholesky)/cholesky | solution.py:56
  637.0 0.3 convolution_dynamic-update-slice_fusion.2
  637.3 1.5 convolution_subtract_fusion.3
  638.8 11.7 %cholesky.390 = f32[128,128]{1,0:T(8,128)S(1)} custom-call(f32[128,128]{1,0:T(8,128)S(1)} %cholesky.440), custom_call_target="Cholesky" | custom-call | tf_op jit(solution)/shard_map/jit(cholesky)/cholesky | solution.py:56
  650.5 0.7 compare_reduce_fusion.1
  651.2 9.8 %custom-call.47 = f32[1,128,128]{1,2,0:T(8,128)S(1)} custom-call(f32[1,128,128]{2,1,0:T(8,128)S(1)} %get-tuple-element.13), custom_call_target="InvertDiagBlocksLowerTriangular" | custom-call | tf_op jit(solution)/shard_map/jit(cholesky)/cholesky | solution.py:56
  661.0 0.2 convolution_dynamic-update-slice_fusion.3
  661.3 1.3 convolution_subtract_fusion.4
  662.6 11.9 %cholesky.408 = f32[128,128]{1,0:T(8,128)S(1)} custom-call(f32[128,128]{1,0:T(8,128)S(1)} %convolution_subtract_fusion.4), custom_call_target="Cholesky" | custom-call | tf_op jit(solution)/shard_map/jit(cholesky)/cholesky | solution.py:56
  674.5 0.7 compare_reduce_fusion
  679.0 0.2 select_select_fusion
  679.2 0.0 copy-done
  679.2 2.9 convolution_bitcast_fusion
  682.2 0.2 dynamic-slice_bitcast_fusion
  682.3 0.9 copy.27
  (14 shorter events, 0.3 us)
Async XLA Ops:
  7.2 672.1 %copy-start = (bf16[1,768,256]{2,1,0:T(8,128)(2,1)S(1)}, bf16[1,768,256]{2,1,0:T(8,128)(2,1)}, u32[]{:S(2)}) copy-start(bf16[1,768,256]{2,1,0:T(8,128)(2,1)} %param.9) | copy-start | bytes 1179652
  7.2 65.8 %all-gather.9.cloned.1.call-start = ((), (), s32[]{:S(2)}) async-start(), calls=%async_computation.2 | async-start | bytes 3538944 | tf_op jit(solution)/shard_map/all_gather | solution.py:50
  7.9 5.0 copy-start.2
  20.3 99.5 %all-to-all-start = ((bf16[4,1,4,128,2048]{4,3,2,1,0:T(8,128)(2,1)}), bf16[4,1,4,128,2048]{4,3,2,1,0:T(8,128)(2,1)}, u32[]{:S(2)}, u32[]{:S(2)}) async-start(bf16[4,1,4,128,2048]{4,3,2,1,0:T(8,128)(2,1)} %bitcast.54), calls=%async_computation | async-start | bytes 16777216 | tf_op jit(solution)/shard_map/all_to_all | solution.py:39
  25.9 107.9 %all-gather.7.cloned.1.call-start = ((), (), s32[]{:S(2)}) async-start(), calls=%async_computation.1 | async-start | bytes 3538944 | tf_op jit(solution)/shard_map/all_gather | solution.py:45
  26.7 498.5 %all-gather.11.cloned.1.call-start = ((), (), s32[]{:S(2)}) async-start(), calls=%async_computation.3 | async-start | bytes 21233664 | tf_op jit(solution)/shard_map/all_gather | solution.py:11
  133.8 10.4 %copy-start.3 = (f32[2048,768]{1,0:T(8,128)S(1)}, f32[2048,768]{1,0:T(8,128)}, u32[]{:S(2)}) copy-start(f32[2048,768]{1,0:T(8,128)} %fusion.7) | copy-start | bytes 18874372
  537.2 1.4 copy-start.1
Sparse Core Ops, SparseCore 0:
  10.2 62.7 all-gather.8
  75.1 58.6 all-gather.6
  163.8 361.3 all-gather.10
